TPU v7x, 32 devices: a whole 2x2x4 slice. The times are simulated.
32 devices in a mesh: groups: 2 (over y), row: 4 (over z), col: 2 (over x), sub: 2 (over core).
Axes of the slice: x: 2, y: 2, z: 4, core: 2. Of those that a mesh axis runs over, the one named last changes fastest.
Arguments:
- query_acts: bfloat16 [64, 128, 4096], P(('groups', 'col', 'sub'), None, 'row'), parts along dimension 0, may hold values from -6 to 6
- query_grads: bfloat16 [64, 128, 4096], P(('groups', 'col', 'sub'), None, 'row'), parts along dimension 0, may hold values from -0.5390625 to 0.5390625
- proj_in: bfloat16 [4096, 128], P('row'), may hold values from -0.09375 to 0.09375
- proj_out: bfloat16 [4096, 128], P('row'), may hold values from -0.09375 to 0.09375
- inverse_gram: float32 [16384, 16384], P('row', ('col', 'sub')), may hold values from -0.01 to 2.01, as said below
- store_slab: bfloat16 [2048, 16384], P(('groups', 'col'), ('row', 'sub')), parts along dimension 0, may hold values from -0.046875 to 0.046875
Outputs:
- scores: float32 [64, 1024], P('groups', 'col'), parts along dimension 0
There are 2 independent parts, one for each index of `groups`. A program takes and returns all parts, laid end to end along the dimension named above; an argument that names none is the same for every part. Nothing has to cross between parts.
Inputs may be any that keep to these rules, and one draw needn't show every extreme that they name: inverse_gram is symmetric.
All inputs are finite; a program needn't handle non-finite values.
Results may differ from a plain program's by a relative error of at most 0.0029.
Values may be sent and summed in bfloat16 or wider, within the bound.
A program may use at most 128 MiB of HBM per device.

v0:
```python
import functools

import jax
import jax.numpy as jnp
from jax import lax
from jax.experimental import pallas as pl
from jax.experimental.pallas import tpu as pltpu
from jax.sharding import PartitionSpec as P

F32, BF16 = jnp.float32, jnp.bfloat16
SLOTS = 11
LAG = 2


def split(x):
    hi = x.astype(BF16)
    return hi, (x - hi.astype(F32)).astype(BF16)


def kernel(rows, cols, subs, acts_h, grads_h, pin_h, pout_h, gram_h, store_h, out,
           acts, grads, pin, pout, gram, store, part, recv, feats, fbuf, ft, pre, sub_in, col_in,
           own, own_s, half_in, half_all, half_out,
           in_sem, gram_sem, rs_send, rs_recv, fx_send, fx_recv, fx_local, fz_send, fz_recv,
           ps_send, ps_recv, pc_send, pc_recv, ss_sem, sz_send, sz_recv, sl_sem, sf_sem):
    g, r, c, s = (lax.axis_index(n) for n in ("groups", "row", "col", "sub"))
    queries = acts.shape[0]
    half = queries // 2
    planes = cols * subs
    me = c * subs + s
    aw = fbuf.shape[2]
    mb, kb = gram.shape[1], gram.shape[2]
    grows, gcols = gram_h.shape
    nk, ni = gcols // kb, grows // mb
    blocks = nk * ni
    per = ni // subs
    other = lax.rem(s + 1, subs)

    def dev(row, col, sub):
        return {"groups": g, "row": row, "col": col, "sub": sub}

    def remote(src, dst, send, rcv, row, col, sub):
        return pltpu.make_async_remote_copy(
            src_ref=src, dst_ref=dst, send_sem=send, recv_sem=rcv,
            device_id=dev(row, col, sub), device_id_type=pl.DeviceIdType.MESH)

    loads = [pltpu.make_async_copy(a, b, in_sem.at[i]) for i, (a, b) in enumerate(
        ((pin_h, pin), (pout_h, pout), (acts_h, acts), (grads_h, grads), (store_h, store)))]
    for l in loads[:4]:
        l.start()

    def gram_copy(b):
        n, k = b // nk, b % nk
        i = lax.rem(other * per + n, ni)
        slot = lax.rem(b, SLOTS)
        return pltpu.make_async_copy(
            gram_h.at[pl.ds(pl.multiple_of(i * mb, mb), mb), pl.ds(pl.multiple_of(k * kb, kb), kb)],
            gram.at[slot], gram_sem.at[slot])

    barrier = pltpu.get_barrier_semaphore()
    count = 0
    for d in range(1, rows):
        pl.semaphore_signal(barrier, inc=1, device_id=dev(lax.rem(r + d, rows), c, s), device_id_type=pl.DeviceIdType.MESH)
        count += 1
    for d in range(1, planes):
        o = lax.rem(me + d, planes)
        pl.semaphore_signal(barrier, inc=1, device_id=dev(r, o // subs, lax.rem(o, subs)), device_id_type=pl.DeviceIdType.MESH)
        count += 1

    def project(q):
        part[q, 0] = jnp.dot(acts[q], pin[...], preferred_element_type=F32)
        part[q, 1] = jnp.dot(grads[q], pout[...], preferred_element_type=F32)

    for l in loads[:4]:
        l.wait()
    for b in range(min(SLOTS, blocks)):
        gram_copy(b).start()
    loads[4].start()
    for q in range(queries):
        project(q)
    pl.semaphore_wait(barrier, count)

    starts = (r == 0, r == rows - 1)
    ends = (r == rows - 1, r == 0)
    ahead = (jnp.minimum(r + 1, rows - 1), jnp.maximum(r - 1, 0))
    behind = (jnp.maximum(r - 1, 0), jnp.minimum(r + 1, rows - 1))

    def rs_copy(h, q, w):
        return remote(part.at[q, w], recv.at[q, w], rs_send.at[q, w], rs_recv.at[q, w], ahead[h], c, s)

    def fx_copy(q, d):
        o = lax.rem(me + d, planes)
        return remote(feats.at[lax.rem(q, half), pl.ds(pl.multiple_of(o * aw, aw), aw)], fbuf.at[me, q],
                      fx_send.at[lax.rem(q, half), d], fx_recv.at[lax.rem(q, half), d], r, o // subs, lax.rem(o, subs))

    def fx_own(q):
        return pltpu.make_async_copy(feats.at[lax.rem(q, half), pl.ds(pl.multiple_of(me * aw, aw), aw)],
                                     fbuf.at[me, q], fx_local.at[lax.rem(q, half)])

    def fz_copy(h, q):
        return remote(fbuf.at[:, q], fbuf.at[:, q], fz_send.at[q], fz_recv.at[q], behind[h], c, s)

    def send_row(h, q):
        for d in range(1, planes):
            fx_copy(q, d).wait()
        fx_own(q).wait()
        fz_copy(h, q).start()

    def sums(t, _):
        for h in range(2):
            j = t - LAG * (r if h == 0 else rows - 1 - r)
            k, w = j // 2, lax.rem(j, 2)
            q = h * half + k
            live = jnp.logical_and(j >= 0, j < 2 * half)

            @pl.when(jnp.logical_and(live, jnp.logical_not(starts[h])))
            def _():
                rs_copy(h, q, w).wait_recv()
                part[q, w] = part[q, w] + recv[q, w]

            @pl.when(jnp.logical_and(live, jnp.logical_not(ends[h])))
            def _():
                rs_copy(h, q, w).start()

            @pl.when(jnp.logical_and(jnp.logical_and(live, ends[h]), w == 1))
            def _():
                feats[k] = jnp.dot(part[q, 0].T, part[q, 1], precision=lax.Precision.HIGHEST,
                                   preferred_element_type=F32)
                for d in range(1, planes):
                    fx_copy(q, d).start()
                fx_own(q).start()

                @pl.when(k > 0)
                def _():
                    send_row(h, q - 1)
        return 0

    lax.fori_loop(0, 2 * half + LAG * (rows - 1), sums, 0)
    for h in range(2):
        @pl.when(ends[h])
        def _():
            send_row(h, h * half + half - 1)

    def back(t, _):
        for h in range(2):
            k = t - LAG * (rows - 1 - r if h == 0 else r)
            q = h * half + k
            live = jnp.logical_and(k >= 0, k < half)

            @pl.when(jnp.logical_and(live, jnp.logical_not(ends[h])))
            def _():
                fz_copy(h, q).wait_recv()

            @pl.when(jnp.logical_and(live, jnp.logical_not(jnp.logical_or(starts[h], ends[h]))))
            def _():
                fz_copy(h, q).start()
        return 0

    lax.fori_loop(0, half + LAG * (rows - 1), back, 0)
    for k in range(half):
        for h in range(2):
            q = h * half + k

            @pl.when(jnp.logical_not(starts[h]))
            def _():
                fz_copy(h, q).wait_send()

            @pl.when(jnp.logical_not(ends[h]))
            def _():
                for w in range(2):
                    rs_copy(h, q, w).wait_send()

    nq = planes * queries
    width = ft.shape[1]
    for a in range(aw):
        x = fbuf[:, :, a, :].reshape(nq, fbuf.shape[3])
        hi, lo = split(x)
        hi, lo = hi.astype(F32), lo.astype(F32)
        rest = [jnp.zeros((width - 2 * nq, x.shape[1]), F32)] if width > 2 * nq else []
        y = jnp.concatenate([hi, lo] + rest, axis=0)
        ft[a * x.shape[1]:(a + 1) * x.shape[1], :] = y.T.astype(BF16)

    step = min(256, mb)

    def sub_copy(p):
        return remote(pre.at[p], sub_in.at[p], ps_send.at[p], ps_recv.at[p], r, c, other)

    def col_copy(p, d):
        return remote(pre.at[per + p], col_in.at[c, p], pc_send.at[d, p], pc_recv.at[d, p], r, lax.rem(c + d, cols), s)

    def block(n, _):
        for k in range(nk):
            gram_copy(n * nk + k).wait()
        for m in range(mb // step):
            acc = None
            for k in range(nk):
                slot = lax.rem(n * nk + k, SLOTS)
                term = jnp.dot(gram[slot, m * step:(m + 1) * step, :].astype(BF16), ft[k * kb:(k + 1) * kb, :],
                               preferred_element_type=F32)
                acc = term if acc is None else acc + term
            t = acc.T
            pre[n, :, m * step:(m + 1) * step] = t[:nq] + t[nq:2 * nq]
        for k in range(nk):
            @pl.when(n * nk + k + SLOTS < blocks)
            def _():
                gram_copy(n * nk + k + SLOTS).start()

        @pl.when(n < per)
        def _():
            sub_copy(n).start()

        @pl.when(n >= per)
        def _():
            sub_copy(n - per).wait_recv()
            pre[n] = pre[n] + sub_in[n - per]
            for d in range(1, cols):
                col_copy(n - per, d).start()
            col_in[c, n - per] = pre[n]
        return 0

    lax.fori_loop(0, ni, block, 0)
    loads[4].wait()
    score = None
    for p in range(per):
        for d in range(1, cols):
            col_copy(p, d).wait()
        sub_copy(p).wait_send()
        total = col_in[0, p]
        for o in range(1, cols):
            total = total + col_in[o, p]
        term = lax.dot_general(jnp.concatenate(split(total), axis=0), store[:, p * mb:(p + 1) * mb],
                               (((1,), (1,)), ((), ())), preferred_element_type=F32)
        score = term if score is None else score + term
    score = score[:nq] + score[nq:]

    hq = nq // subs
    for o in range(subs):
        own[o] = score[o * hq:(o + 1) * hq]
    x_half = remote(own.at[other], half_in, ss_sem.at[0], ss_sem.at[1], r, c, other)
    x_half.start()
    x_half.wait()
    own_s[...] = own[s] + half_in[...]
    x_rows = [remote(own_s, half_all.at[r], sz_send.at[d], sz_recv.at[d], lax.rem(r + d, rows), c, s)
              for d in range(1, rows)]
    for x in x_rows:
        x.start()
    half_all[r] = own_s[...]
    for x in x_rows:
        x.wait()
    total = half_all[0]
    for o in range(1, rows):
        total = total + half_all[o]
    half_out[s] = total
    x_out = remote(half_out.at[s], half_out.at[s], sf_sem.at[0], sf_sem.at[1], r, c, other)
    x_out.start()
    x_out.wait()
    for o in range(subs):
        out[o * hq:(o + 1) * hq, :] = half_out[o]


def body(sizes, query_acts, query_grads, proj_in, proj_out, inverse_gram, store_slab):
    rows, cols, subs = sizes
    queries, tokens, depth = query_acts.shape
    kin, kout = proj_in.shape[1], proj_out.shape[1]
    planes = cols * subs
    nq = planes * queries
    aw = kin // planes
    grows, gcols = inverse_gram.shape
    mb, kb = min(512, grows // subs), min(2048, gcols)
    per = grows // subs // mb
    examples, width = store_slab.shape
    half = queries // 2
    hq = nq // subs
    dma = pltpu.SemaphoreType.DMA
    lanes = -(-2 * nq // 128) * 128
    scratch = [
        pltpu.VMEM(query_acts.shape, BF16), pltpu.VMEM(query_grads.shape, BF16),
        pltpu.VMEM(proj_in.shape, BF16), pltpu.VMEM(proj_out.shape, BF16),
        pltpu.VMEM((SLOTS, mb, kb), F32), pltpu.VMEM(store_slab.shape, BF16),
        pltpu.VMEM((queries, 2, tokens, kin), F32), pltpu.VMEM((queries, 2, tokens, kin), F32),
        pltpu.VMEM((half, kin, kout), F32), pltpu.VMEM((planes, queries, aw, kout), F32),
        pltpu.VMEM((gcols, lanes), BF16),
        pltpu.VMEM((subs * per, nq, mb), F32), pltpu.VMEM((per, nq, mb), F32),
        pltpu.VMEM((cols, per, nq, mb), F32),
        pltpu.VMEM((subs, hq, examples), F32), pltpu.VMEM((hq, examples), F32), pltpu.VMEM((hq, examples), F32),
        pltpu.VMEM((rows, hq, examples), F32), pltpu.VMEM((subs, hq, examples), F32),
        dma((5,)), dma((SLOTS,)), dma((queries, 2)), dma((queries, 2)),
        dma((half, planes)), dma((half, planes)), dma((half,)), dma((queries,)), dma((queries,)),
        dma((per,)), dma((per,)), dma((cols, per)), dma((cols, per)), dma((2,)), dma((rows,)), dma((rows,)), dma((1,)), dma((2,)),
    ]
    return pl.pallas_call(
        functools.partial(kernel, rows, cols, subs),
        out_shape=jax.ShapeDtypeStruct((nq, examples), F32),
        in_specs=[pl.BlockSpec(memory_space=pltpu.HBM)] * 6,
        out_specs=pl.BlockSpec(memory_space=pltpu.VMEM),
        scratch_shapes=scratch,
        compiler_params=pltpu.CompilerParams(
            collective_id=0, has_side_effects=True, vmem_limit_bytes=67043328),
        name="influence",
    )(query_acts, query_grads, proj_in, proj_out, inverse_gram, store_slab)


def solution(mesh):
    sizes = (mesh.shape["row"], mesh.shape["col"], mesh.shape["sub"])
    return jax.shard_map(
        functools.partial(body, sizes),
        mesh=mesh,
        in_specs=(
            P(("groups", "col", "sub"), None, "row"),
            P(("groups", "col", "sub"), None, "row"),
            P("row", None),
            P("row", None),
            P("row", ("col", "sub")),
            P(("groups", "col"), ("row", "sub")),
        ),
        out_specs=P("groups", "col"),
        check_vma=False,
    )
```

profile of v0, /device:TPU:0, one launch (start us, length us, event | category | flops | bytes accessed | tf_op | source)
XLA Modules:
  0.0 65.8 jit_solution(12338989482371889737)
XLA Ops:
  0.0 64.4 %influence.1 = f32[32,512]{1,0:T(8,128)} custom-call(bf16[8,128,1024]{2,1,0:T(8,128)(2,1)} %acts_h.1, bf16[8,128,1024]{2,1,0:T(8,128)(2,1)} %grads_h.1, bf16[1024,128]{1,0:T(8,128)(2,1)} %pin_h.1, bf16[1024,128]{1,0:T(8,128)(2,1)} %pout_h.1, f32[4096,4096]{1,0:T(8,128)} %gram_h.1, bf16[512,2048]{1,0:T(8,128)(2,1)} %store_h.1), custom_call_target="tpu_custom_call" | custom-call | tf_op jit(solution)/shard_map/influence/pallas_call | solution.py:290
  64.4 1.5 %copy.8 = f32[32,512]{1,0:T(8,128)} copy(f32[32,512]{1,0:T(8,128)} %influence.1) | data formatting | bytes 131072
where the time goes:
time: 66 us; the launch traced here: 65.8 us
  Pallas kernels  64.4 us (98%)
  local copies, waits for them, and re-layouts  1.47 us (2%)
    pallas_call x1, Pallas kernels, body(): pl.pallas_call(functools.partial(kernel, rows, cols, subs), out_shape=jax...  64.4 us
    unnamed x1, local copies, waits for them, and re-layouts  1.47 us

commit v1 on v0

v1 whole, which is shorter than its diff:
```python
import functools
import math

import jax
import jax.numpy as jnp
from jax import lax
from jax.experimental import pallas as pl
from jax.experimental.pallas import tpu as pltpu
from jax.sharding import PartitionSpec as P

F32, BF16 = jnp.float32, jnp.bfloat16
LAG = 3
ACT_MAX, GRAD_MAX, PROJ_MAX, GRAM_MAX = 6.0, 0.5390625, 0.09375, 2.01


def split(x):
    hi = x.astype(BF16)
    return hi, (x - hi.astype(F32)).astype(BF16)


def scale_of(p, bound):
    return 2.0 ** math.floor(126 / p - math.log2(bound))


def encode(x, p, scale):
    z = x * scale
    if p == 2:
        y = z * jnp.abs(z)
    elif p == 3:
        y = z * z * z
    else:
        y = (z * z) * (z * jnp.abs(z))
    return y.astype(BF16)


def decode(y, p, scale):
    y = y.astype(F32)
    m = jnp.abs(y)
    if p == 2:
        v = m * lax.rsqrt(m) * (1.0 / scale)
    elif p == 3:
        v = jnp.exp2(jnp.log2(m) * (1.0 / 3.0)) * (1.0 / scale)
    else:
        v = lax.rsqrt(lax.rsqrt(m)) * (1.0 / scale)
    return jnp.where(y > 0, v, jnp.where(y < 0, -v, 0.0))


def kernel(groups, rows, cols, subs, acts_h, grads_h, pin_h, pout_h, gram_h, store_h, out,
           acts, grads, pin, pout, gram, store, part, send, recv, fsend, fbuf, feats, ft,
           pre, sub_in, tot, ysend, yin, xsend, xin,
           own, own_s, half_in, half_all, half_out,
           p_sem, in_sem, gram_sem, store_sem, rs_send, rs_recv, fx_send, fx_recv, fx_local, fz_send, fz_recv,
           ps_send, ps_recv, py_send, py_recv, pc_send, pc_recv, ss_sem, sz_send, sz_recv, sf_sem):
    g, r, c, s = (lax.axis_index(n) for n in ("groups", "row", "col", "sub"))
    queries, tokens, depth = acts.shape
    planes = cols * subs
    slices = groups * planes
    me = c * subs + s
    spot = me * groups + g
    source = g * planes + me
    aw, kout = feats.shape[2], feats.shape[3]
    blocks, mb, kw = gram.shape
    per = blocks // subs
    other = lax.rem(s + 1, subs)
    nq = planes * queries
    homes = -(-queries // rows)
    act_bound = rows * depth * ACT_MAX * PROJ_MAX
    grad_bound = rows * depth * GRAD_MAX * PROJ_MAX
    feat_bound = tokens * act_bound * grad_bound
    ps = scale_of(4, max(act_bound, grad_bound))
    fs = scale_of(3, feat_bound)
    gs = scale_of(2, feat_bound * GRAM_MAX * gram_h.shape[1] * planes)

    def dev(group, row, col, sub):
        return {"groups": group, "row": row, "col": col, "sub": sub}

    def remote(src, dst, snd, rcv, group, row, col, sub):
        return pltpu.make_async_remote_copy(
            src_ref=src, dst_ref=dst, send_sem=snd, recv_sem=rcv,
            device_id=dev(group, row, col, sub), device_id_type=pl.DeviceIdType.MESH)

    def at_spot(o):
        plane = o // groups
        return lax.rem(o, groups), r, plane // subs, lax.rem(plane, subs)

    def first(row):
        return (row * queries + rows - 1) // rows

    lo, hi = first(r), first(r + 1)
    lower, upper = jnp.maximum(r - 1, 0), jnp.minimum(r + 1, rows - 1)

    loads = [pltpu.make_async_copy(pin_h, pin, p_sem.at[0]), pltpu.make_async_copy(pout_h, pout, p_sem.at[1])]
    for l in loads:
        l.start()

    def pick(i):
        return jnp.where(2 * r < rows, queries - 1 - i, i)

    def load(i):
        q = pick(i)
        return (pltpu.make_async_copy(acts_h.at[q], acts.at[q], in_sem.at[q, 0]),
                pltpu.make_async_copy(grads_h.at[q], grads.at[q], in_sem.at[q, 1]))

    for i in range(queries):
        for l in load(i):
            l.start()

    def gram_copy(n):
        i = lax.rem(other * per + n, blocks)
        return pltpu.make_async_copy(
            gram_h.at[pl.ds(pl.multiple_of(i * mb, mb), mb), pl.ds(pl.multiple_of(g * kw, kw), kw)],
            gram.at[n], gram_sem.at[n])

    store_copy = pltpu.make_async_copy(store_h, store, store_sem.at[0])

    barrier = pltpu.get_barrier_semaphore()
    for d in range(1, rows):
        pl.semaphore_signal(barrier, inc=1, device_id=dev(g, lax.rem(r + d, rows), c, s),
                            device_id_type=pl.DeviceIdType.MESH)
    for d in range(1, slices):
        pl.semaphore_signal(barrier, inc=1, device_id=dev(*at_spot(lax.rem(spot + d, slices))),
                            device_id_type=pl.DeviceIdType.MESH)

    def rs_copy(side, q, w):
        return remote(send.at[q, w], recv.at[side, q, w], rs_send.at[q, w], rs_recv.at[side, q, w],
                      g, lower if side else upper, c, s)

    def pass_on(side, q, w, value):
        send[q, w] = encode(value, 4, ps)
        rs_copy(side, q, w).start()

    for l in loads:
        l.wait()
    pl.semaphore_wait(barrier, rows - 1 + slices - 1)

    def project(i, _):
        q = pick(i)
        for w, (l, x, y) in enumerate(zip(load(i), (acts, grads), (pin, pout))):
            l.wait()
            value = jnp.dot(x[q], y[...], preferred_element_type=F32)
            part[q, w] = value

            @pl.when(jnp.logical_and(r == 0, q >= hi))
            def _():
                pass_on(0, q, w, value)

            @pl.when(jnp.logical_and(r == rows - 1, q < lo))
            def _():
                pass_on(1, q, w, value)
        return 0

    lax.fori_loop(0, queries, project, 0)
    for n in range(blocks):
        gram_copy(n).start()
    store_copy.start()

    def fx_copy(i, d):
        o = lax.rem(spot + d, slices)
        return remote(fsend.at[i, o], fbuf.at[lo + i, source], fx_send.at[i, d], fx_recv.at[i, d], *at_spot(o))

    def fx_own(i):
        return pltpu.make_async_copy(fsend.at[i, spot], fbuf.at[lo + i, source], fx_local.at[i])

    def fz_copy(side, q):
        return remote(fbuf.at[q], fbuf.at[q], fz_send.at[side, q], fz_recv.at[q],
                      g, lower if side else upper, c, s)

    def sums(t, _):
        for side in range(2):
            j = t - LAG * (rows - 1 - r if side else r)
            w = lax.rem(j, 2)
            q = j // 2 if side else queries - 1 - j // 2
            if side:
                live = jnp.logical_and(r < rows - 1, jnp.logical_and(j >= 0, q < hi))
                onward = q < lo
            else:
                live = jnp.logical_and(r > 0, jnp.logical_and(j >= 0, q >= lo))
                onward = q >= hi

            @pl.when(live)
            def _():
                rs_copy(side, q, w).wait_recv()
                value = part[q, w] + decode(recv[side, q, w], 4, ps)

                @pl.when(onward)
                def _():
                    pass_on(side, q, w, value)

                @pl.when(jnp.logical_not(onward))
                def _():
                    part[q, w] = value

        for i in range(homes):
            q = lo + i
            up = jnp.where(r > 0, LAG * r + 2 * (queries - 1 - q) + 1, 0)
            down = jnp.where(r < rows - 1, LAG * (rows - 1 - r) + 2 * q + 1, 0)

            @pl.when(jnp.logical_and(q < hi, t == jnp.maximum(up, down)))
            def _():
                ah, al = split(part[q, 0].T)
                gh, gl = split(part[q, 1])
                f = jnp.dot(jnp.concatenate([ah, al, ah], axis=1), jnp.concatenate([gh, gh, gl], axis=0),
                            preferred_element_type=F32)
                fsend[i] = encode(f.reshape(slices, aw, kout), 3, fs)
                for d in range(1, slices):
                    fx_copy(i, d).start()
                fx_own(i).start()
        return 0

    span = max(LAG * k + 2 * (queries - -(-k * queries // rows)) for k in range(rows))
    lax.fori_loop(LAG, span, sums, 0)

    def unpack(q):
        feats[:, q] = decode(fbuf[q], 3, fs)

    for i in range(homes):
        @pl.when(lo + i < hi)
        def _():
            for d in range(1, slices):
                fx_copy(i, d).wait_recv()
            fx_own(i).wait()

            @pl.when(r < rows - 1)
            def _():
                fz_copy(0, lo + i).start()

            @pl.when(r > 0)
            def _():
                fz_copy(1, lo + i).start()
            unpack(lo + i)

    def gather(d, _):
        for i in range(homes):
            for side in range(2):
                h = r + d if side else r - d
                q = first(h) + i

                @pl.when(jnp.logical_and(jnp.logical_and(h >= 0, h < rows), q < first(h + 1)))
                def _():
                    fz_copy(side, q).wait_recv()

                    @pl.when((r > 0) if side else (r < rows - 1))
                    def _():
                        fz_copy(side, q).start()
                    unpack(q)
        return 0

    lax.fori_loop(1, rows, gather, 0)

    width = ft.shape[1]
    allq = groups * nq
    for a in range(aw):
        x = feats[:, :, a, :].reshape(allq, kout)
        xh, xl = split(x)
        rest = [jnp.zeros((width - 2 * allq, kout), F32)] if width > 2 * allq else []
        y = jnp.concatenate([xh.astype(F32), xl.astype(F32)] + rest, axis=0)
        ft[a * kout:(a + 1) * kout, :] = y.T.astype(BF16)

    def sub_copy(p):
        return remote(pre.at[p], sub_in.at[p], ps_send.at[p], ps_recv.at[p], g, r, c, other)

    def y_copy(p, d):
        o = lax.rem(g + d, groups)
        return remote(ysend.at[p, o], yin.at[p, d], py_send.at[p, d], py_recv.at[p, d], o, r, c, s)

    def x_copy(p, d):
        return remote(xsend.at[p], xin.at[p, d], pc_send.at[p, d], pc_recv.at[p, d], g, r, lax.rem(c + d, cols), s)

    def product(n):
        gram_copy(n).wait()
        acc = jnp.dot(gram[n].astype(BF16), ft[...], preferred_element_type=F32)
        t = acc.T
        return t[:allq] + t[allq:2 * allq]

    for n in range(per):
        pre[n] = product(n)
        for k in range(subs - 1):
            sub_copy(n).start()

    def give(p):
        value = product(per + p)
        sub_copy(p).wait_recv()
        value = (value + sub_in[p]).reshape(groups, nq, mb)
        tot[p] = value
        ysend[p] = encode(value, 2, gs)
        for d in range(1, groups):
            y_copy(p, d).start()

    def across(p):
        value = tot[p, g]
        for d in range(1, groups):
            y_copy(p, d).wait_recv()
            value = value + decode(yin[p, d], 2, gs)
        tot[p, g] = value
        xsend[p] = encode(value, 2, gs)
        for d in range(1, cols):
            x_copy(p, d).start()

    def score_of(p):
        value = tot[p, g]
        for d in range(1, cols):
            x_copy(p, d).wait_recv()
            value = value + decode(xin[p, d], 2, gs)
        return lax.dot_general(jnp.concatenate(split(value), axis=0), store[:, p * mb:(p + 1) * mb],
                               (((1,), (1,)), ((), ())), preferred_element_type=F32)

    for p in range(per):
        give(p)
    store_copy.wait()
    for p in range(per):
        across(p)
    score = None
    for p in range(per):
        term = score_of(p)
        score = term if score is None else score + term
    score = score[:nq] + score[nq:]

    hq = nq // subs
    for o in range(subs):
        own[o] = score[o * hq:(o + 1) * hq]
    x_half = remote(own.at[other], half_in, ss_sem.at[0], ss_sem.at[1], g, r, c, other)
    x_half.start()
    x_half.wait()
    own_s[...] = own[s] + half_in[...]
    x_rows = [remote(own_s, half_all.at[r], sz_send.at[d], sz_recv.at[d], g, lax.rem(r + d, rows), c, s)
              for d in range(1, rows)]
    for x in x_rows:
        x.start()
    half_all[r] = own_s[...]
    for x in x_rows:
        x.wait()
    total = half_all[0]
    for o in range(1, rows):
        total = total + half_all[o]
    half_out[s] = total
    x_out = remote(half_out.at[s], half_out.at[s], sf_sem.at[0], sf_sem.at[1], g, r, c, other)
    x_out.start()

    for p in range(per):
        sub_copy(p).wait_send()
        for d in range(1, groups):
            y_copy(p, d).wait_send()
        for d in range(1, cols):
            x_copy(p, d).wait_send()
    for i in range(homes):
        @pl.when(lo + i < hi)
        def _():
            for d in range(1, slices):
                fx_copy(i, d).wait_send()

    def drain(q, _):
        @pl.when(jnp.logical_and(r < rows - 1, q < hi))
        def _():
            fz_copy(0, q).wait_send()

        @pl.when(jnp.logical_and(r > 0, q >= lo))
        def _():
            fz_copy(1, q).wait_send()

        for side, gone in enumerate((q >= hi, q < lo)):
            @pl.when(gone)
            def _():
                for w in range(2):
                    rs_copy(side, q, w).wait_send()
        return 0

    lax.fori_loop(0, queries, drain, 0)
    x_out.wait()
    for o in range(subs):
        out[o * hq:(o + 1) * hq, :] = half_out[o]


def body(sizes, query_acts, query_grads, proj_in, proj_out, inverse_gram, store_slab):
    groups, rows, cols, subs = sizes
    queries, tokens, depth = query_acts.shape
    kin, kout = proj_in.shape[1], proj_out.shape[1]
    planes = cols * subs
    slices = groups * planes
    nq = planes * queries
    aw = kin // slices
    grows, gcols = inverse_gram.shape
    kw = gcols // groups
    mb = min(512, grows // subs)
    blocks = grows // mb
    per = blocks // subs
    examples = store_slab.shape[0]
    hq = nq // subs
    homes = -(-queries // rows)
    dma = pltpu.SemaphoreType.DMA
    lanes = -(-2 * groups * nq // 128) * 128
    scratch = [
        pltpu.VMEM(query_acts.shape, BF16), pltpu.VMEM(query_grads.shape, BF16),
        pltpu.VMEM(proj_in.shape, BF16), pltpu.VMEM(proj_out.shape, BF16),
        pltpu.VMEM((blocks, mb, kw), F32), pltpu.VMEM(store_slab.shape, BF16),
        pltpu.VMEM((queries, 2, tokens, kin), F32), pltpu.VMEM((queries, 2, tokens, kin), BF16),
        pltpu.VMEM((2, queries, 2, tokens, kin), BF16),
        pltpu.VMEM((homes, slices, aw, kout), BF16), pltpu.VMEM((queries, slices, aw, kout), BF16),
        pltpu.VMEM((slices, queries, aw, kout), F32), pltpu.VMEM((kw, lanes), BF16),
        pltpu.VMEM((per, groups * nq, mb), F32), pltpu.VMEM((per, groups * nq, mb), F32),
        pltpu.VMEM((per, groups, nq, mb), F32),
        pltpu.VMEM((per, groups, nq, mb), BF16), pltpu.VMEM((per, groups, nq, mb), BF16),
        pltpu.VMEM((per, nq, mb), BF16), pltpu.VMEM((per, cols, nq, mb), BF16),
        pltpu.VMEM((subs, hq, examples), F32), pltpu.VMEM((hq, examples), F32), pltpu.VMEM((hq, examples), F32),
        pltpu.VMEM((rows, hq, examples), F32), pltpu.VMEM((subs, hq, examples), F32),
        dma((2,)), dma((queries, 2)), dma((blocks,)), dma((1,)), dma((queries, 2)), dma((2, queries, 2)),
        dma((homes, slices)), dma((homes, slices)), dma((homes,)), dma((2, queries)), dma((queries,)),
        dma((per,)), dma((per,)), dma((per, groups)), dma((per, groups)), dma((per, cols)), dma((per, cols)),
        dma((2,)), dma((rows,)), dma((rows,)), dma((2,)),
    ]
    return pl.pallas_call(
        functools.partial(kernel, groups, rows, cols, subs),
        out_shape=jax.ShapeDtypeStruct((nq, examples), F32),
        in_specs=[pl.BlockSpec(memory_space=pltpu.HBM)] * 6,
        out_specs=pl.BlockSpec(memory_space=pltpu.VMEM),
        scratch_shapes=scratch,
        compiler_params=pltpu.CompilerParams(
            collective_id=0, has_side_effects=True, vmem_limit_bytes=67043328),
        name="influence",
    )(query_acts, query_grads, proj_in, proj_out, inverse_gram, store_slab)


def solution(mesh):
    sizes = tuple(mesh.shape[n] for n in ("groups", "row", "col", "sub"))
    return jax.shard_map(
        functools.partial(body, sizes),
        mesh=mesh,
        in_specs=(
            P(("groups", "col", "sub"), None, "row"),
            P(("groups", "col", "sub"), None, "row"),
            P("row", None),
            P("row", None),
            P("row", ("col", "sub")),
            P(("groups", "col"), ("row", "sub")),
        ),
        out_specs=P("groups", "col"),
        check_vma=False,
    )
```

time: 66 us -> 58.4 us (0.88)
  Pallas kernels: 64.4 us -> 56.8 us
    pallas_call x1, Pallas kernels: 64.4 us -> 56.8 us  [body(): pl.pallas_call(functools.partial(kernel, groups, rows, cols, subs), out_s...]
where the time goes in v1:
time: 58.4 us; the launch traced here: 58.2 us
  Pallas kernels  56.8 us (97%)
  local copies, waits for them, and re-layouts  1.47 us (3%)
    pallas_call x1, Pallas kernels, body(): pl.pallas_call(functools.partial(kernel, groups, rows, cols, subs), out_s...  56.8 us
    unnamed x1, local copies, waits for them, and re-layouts  1.47 us

profile of v1, /device:TPU:0, one launch (start us, length us, event | category | flops | bytes accessed | tf_op | source)
XLA Modules:
  0.0 58.2 jit_solution(13746149837212693945)
XLA Ops:
  0.0 56.8 %influence.1 = f32[32,512]{1,0:T(8,128)} custom-call(bf16[8,128,1024]{2,1,0:T(8,128)(2,1)} %acts_h.1, bf16[8,128,1024]{2,1,0:T(8,128)(2,1)} %grads_h.1, bf16[1024,128]{1,0:T(8,128)(2,1)} %pin_h.1, bf16[1024,128]{1,0:T(8,128)(2,1)} %pout_h.1, f32[4096,4096]{1,0:T(8,128)} %gram_h.1, bf16[512,2048]{1,0:T(8,128)(2,1)} %store_h.1), custom_call_target="tpu_custom_call" | custom-call | tf_op jit(solution)/shard_map/influence/pallas_call | solution.py:410
  56.8 1.5 %copy.8 = f32[32,512]{1,0:T(8,128)} copy(f32[32,512]{1,0:T(8,128)} %influence.1) | data formatting | bytes 131072

commit v2 on v1

v2 whole, which is shorter than its diff:
```python
import functools
import math

import jax
import jax.numpy as jnp
from jax import lax
from jax.experimental import pallas as pl
from jax.experimental.pallas import tpu as pltpu
from jax.sharding import PartitionSpec as P

F32, BF16 = jnp.float32, jnp.bfloat16
ACT_MAX, GRAD_MAX, PROJ_MAX, GRAM_MAX = 6.0, 0.5390625, 0.09375, 2.01


def split(x):
    hi = x.astype(BF16)
    return hi, (x - hi.astype(F32)).astype(BF16)


def scale_of(p, bound):
    return 2.0 ** math.floor(126 / p - math.log2(bound))


def encode(x, p, scale):
    z = x * scale
    if p == 2:
        y = z * jnp.abs(z)
    elif p == 3:
        y = z * z * z
    else:
        y = (z * z) * (z * jnp.abs(z))
    return y.astype(BF16)


def decode(y, p, scale):
    y = y.astype(F32)
    m = jnp.abs(y)
    if p == 2:
        v = m * lax.rsqrt(m) * (1.0 / scale)
    elif p == 3:
        v = jnp.exp2(jnp.log2(m) * (1.0 / 3.0)) * (1.0 / scale)
    else:
        v = lax.rsqrt(lax.rsqrt(m)) * (1.0 / scale)
    return jnp.where(y > 0, v, jnp.where(y < 0, -v, 0.0))


def each(n, fn):
    if n <= 8:
        for i in range(n):
            fn(i)
    else:
        def step(i, _):
            fn(i)
            return 0
        lax.fori_loop(0, n, step, 0)


def kernel(groups, rows, cols, subs, acts_h, grads_h, pin_h, pout_h, gram_h, store_h, out,
           acts, grads, pin, pout, gram, store, part, send, relay, recv, fsend, fbuf, feats, ft,
           pre, sub_in, tot, vsend, vin, own, own_s, half_in, half_all, half_out,
           p_sem, in_sem, gram_sem, store_sem, rs_send, rl_recv, rh_recv, fx_send, fx_recv,
           ps_send, ps_recv, pv_send, pv_recv, ss_sem, sz_send, sz_recv, sf_sem):
    g, r, c, s = (lax.axis_index(n) for n in ("groups", "row", "col", "sub"))
    queries, tokens, depth = acts.shape
    planes = cols * subs
    slices = groups * planes
    me = c * subs + s
    spot = me * groups + g
    source = g * planes + me
    aw, kout = feats.shape[2], feats.shape[3]
    kin = pin.shape[1]
    blocks, mb, kw = gram.shape
    per = blocks // subs
    other = lax.rem(s + 1, subs)
    nq = planes * queries
    homes = fsend.shape[0]
    act_bound = rows * depth * ACT_MAX * PROJ_MAX
    grad_bound = rows * depth * GRAD_MAX * PROJ_MAX
    feat_bound = tokens * act_bound * grad_bound
    ps = scale_of(4, max(act_bound, grad_bound))
    fs = scale_of(3, feat_bound)
    gs = scale_of(2, feat_bound * GRAM_MAX * gram_h.shape[1] * planes)

    def dev(group, row, col, sub):
        return {"groups": group, "row": row, "col": col, "sub": sub}

    def remote(src, dst, snd, rcv, group, row, col, sub):
        return pltpu.make_async_remote_copy(
            src_ref=src, dst_ref=dst, send_sem=snd, recv_sem=rcv,
            device_id=dev(group, row, col, sub), device_id_type=pl.DeviceIdType.MESH)

    def at_spot(o, row):
        plane = o // groups
        return lax.rem(o, groups), row, plane // subs, lax.rem(plane, subs)

    def first(row):
        return (row * queries + rows - 1) // rows

    def when_some(h, fn):
        def run():
            fn()

        if queries % rows == 0:
            run()
        else:
            pl.when(first(h) < first(h + 1))(run)

    odd = lax.rem(r, 2)
    pair = r // 2
    partner = r + 1 - 2 * odd

    def target(i):
        h = jnp.where(odd == 1, jnp.where(i < r, i, rows - 1 - i + r),
                      jnp.where(i < rows - 1 - r, rows - 1 - i, i - (rows - 1 - r)))
        return jnp.where(i == rows - 1, r, h)

    def relays(h):
        return jnp.where(odd == 1, h > r, h < r)

    loads = [pltpu.make_async_copy(pin_h, pin, p_sem.at[0]), pltpu.make_async_copy(pout_h, pout, p_sem.at[1])]

    def load(h, w):
        q = pl.ds(first(h), homes)
        return pltpu.make_async_copy((acts_h, grads_h)[w].at[q], (acts, grads)[w].at[q], in_sem.at[h, w])

    for w in range(2):
        loads[w].start()
        when_some(target(0), lambda: load(target(0), w).start())

    def more(i):
        h = target(i + 1)
        when_some(h, lambda: [load(h, w).start() for w in range(2)])

    each(rows - 1, more)

    def gram_copy(n):
        i = (other if n % subs == 0 else s) * per + n // subs
        return pltpu.make_async_copy(
            gram_h.at[pl.ds(pl.multiple_of(i * mb, mb), mb), pl.ds(pl.multiple_of(g * kw, kw), kw)],
            gram.at[n], gram_sem.at[n])

    store_copy = pltpu.make_async_copy(store_h, store, store_sem.at[0])

    barrier = pltpu.get_barrier_semaphore()
    everyone = rows * slices

    def greet(d):
        o = lax.rem(r * slices + spot + d + 1, everyone)
        group, row, col, sub = at_spot(lax.rem(o, slices), o // slices)
        pl.semaphore_signal(barrier, inc=1, device_id=dev(group, row, col, sub), device_id_type=pl.DeviceIdType.MESH)

    lax.fori_loop(0, everyone - 1, lambda d, z: (greet(d), z)[1], 0)

    def relay_copy(w, q):
        return remote(send.at[w, q], relay.at[w, q], rs_send.at[w, q], rl_recv.at[w, q], g, partner, c, s)

    def home_copy(w, h, k):
        q = first(h) + k
        return remote(send.at[w, q], recv.at[pair, w, k], rs_send.at[w, q], rh_recv.at[pair, w, k], g, h, c, s)

    def project(i):
        h = target(i)

        def _():
            q = pl.ds(first(h), homes)
            for w, (x, y) in enumerate(((acts, pin), (grads, pout))):
                if isinstance(i, int) and i == 0:
                    loads[w].wait()
                load(h, w).wait()
                value = jnp.dot(x[q].reshape(homes * tokens, depth), y[...],
                                preferred_element_type=F32).reshape(homes, tokens, kin)
                part[w, q] = value
                if isinstance(i, int) and i == 0 and w == 0:
                    pl.semaphore_wait(barrier, everyone - 1)

                @pl.when(jnp.logical_not(jnp.logical_or(h == r, relays(h))))
                def _():
                    send[w, q] = encode(value, 4, ps)
                    for k in range(homes):
                        @pl.when(h == partner)
                        def _():
                            home_copy(w, h, k).start()

                        @pl.when(h != partner)
                        def _():
                            relay_copy(w, first(h) + k).start()

        when_some(h, _)

    if rows > 8:
        for l in loads:
            l.wait()
        pl.semaphore_wait(barrier, everyone - 1)
    each(rows, project)
    for n in range(blocks):
        gram_copy(n).start()
    store_copy.start()

    def forward(i):
        h = target(i)

        def _():
            @pl.when(relays(h))
            def _():
                for w in range(2):
                    for k in range(homes):
                        q = first(h) + k
                        relay_copy(w, q).wait_recv()
                        send[w, q] = encode(part[w, q] + decode(relay[w, q], 4, ps), 4, ps)
                        home_copy(w, h, k).start()

        @pl.when(h != partner)
        def _():
            when_some(h, _)

    each(rows - 1, forward)

    def fx_copy(k, row, o):
        return remote(fsend.at[k, o], fbuf.at[first(r) + k, source], fx_send.at[k, row, o],
                      fx_recv.at[first(r) + k], *at_spot(o, row))

    def fx_own(k):
        return pltpu.make_async_copy(fsend.at[k, spot], fbuf.at[first(r) + k, source], fx_recv.at[first(r) + k])

    def users(k, use):
        def row_of(j):
            row = jnp.where(2 * r < rows, rows - 1 - j, j)

            def slice_of(d):
                o = lax.rem(spot + d, slices)

                @pl.when(jnp.logical_or(row != r, o != spot))
                def _():
                    use(fx_copy(k, row, o))

            each(slices, slice_of)

        each(rows, row_of)

    def final():
        for k in range(homes):
            q = first(r) + k
            sides = []
            for w in range(2):
                value = part[w, q]
                for o in range(rows // 2):
                    remote(send.at[w, q], recv.at[o, w, k], rs_send.at[w, q], rh_recv.at[o, w, k],
                           g, partner, c, s).wait_recv()
                    value = value + decode(recv[o, w, k], 4, ps)
                sides.append(value)
            ah, al = split(sides[0].T)
            gh, gl = split(sides[1])
            f = jnp.dot(jnp.concatenate([ah, al, ah], axis=1), jnp.concatenate([gh, gh, gl], axis=0),
                        preferred_element_type=F32)
            fsend[k] = encode(f.reshape(slices, aw, kout), 3, fs)
            users(k, lambda copy: copy.start())
            fx_own(k).start()

    when_some(r, final)

    for q in range(queries):
        remote(fbuf.at[q], fbuf.at[q], fx_send.at[0, 0, 0], fx_recv.at[q], g, partner, c, s).wait_recv()
        feats[:, q] = decode(fbuf[q], 3, fs)

    width = ft.shape[1]
    allq = groups * nq
    for a in range(aw):
        x = feats[:, :, a, :].reshape(allq, kout)
        xh, xl = split(x)
        rest = [jnp.zeros((width - 2 * allq, kout), F32)] if width > 2 * allq else []
        y = jnp.concatenate([xh.astype(F32), xl.astype(F32)] + rest, axis=0)
        ft[a * kout:(a + 1) * kout, :] = y.T.astype(BF16)

    def sub_copy(p):
        return remote(pre.at[p], sub_in.at[p], ps_send.at[p], ps_recv.at[p], g, r, c, other)

    spread = groups * cols
    mine = g * cols + c

    def v_copy(p, d):
        o = lax.rem(mine + d, spread)
        return remote(vsend.at[p, o // cols], vin.at[p, d], pv_send.at[p, d], pv_recv.at[p, d],
                      o // cols, r, lax.rem(o, cols), s)

    def product(n):
        gram_copy(n).wait()
        acc = jnp.dot(gram[n].astype(BF16), ft[...], preferred_element_type=F32)
        t = acc.T
        return t[:allq] + t[allq:2 * allq]

    for p in range(per):
        pre[p] = product(subs * p)
        sub_copy(p).start()
        value = product(subs * p + 1)
        sub_copy(p).wait_recv()
        value = (value + sub_in[p]).reshape(groups, nq, mb)
        tot[p] = value
        vsend[p] = encode(value, 2, gs)
        for d in range(1, spread):
            v_copy(p, d).start()
    store_copy.wait()
    score = None
    for p in range(per):
        value = tot[p, g]
        for d in range(1, spread):
            v_copy(p, d).wait_recv()
            value = value + decode(vin[p, d], 2, gs)
        term = lax.dot_general(jnp.concatenate(split(value), axis=0), store[:, p * mb:(p + 1) * mb],
                               (((1,), (1,)), ((), ())), preferred_element_type=F32)
        score = term if score is None else score + term
    score = score[:nq] + score[nq:]

    hq = nq // subs
    for o in range(subs):
        own[o] = score[o * hq:(o + 1) * hq]
    x_half = remote(own.at[other], half_in, ss_sem.at[0], ss_sem.at[1], g, r, c, other)
    x_half.start()
    x_half.wait()
    own_s[...] = own[s] + half_in[...]
    x_rows = [remote(own_s, half_all.at[r], sz_send.at[d], sz_recv.at[d], g, lax.rem(r + d, rows), c, s)
              for d in range(1, rows)]
    for x in x_rows:
        x.start()
    half_all[r] = own_s[...]
    for p in range(per):
        sub_copy(p).wait_send()
        for d in range(1, spread):
            v_copy(p, d).wait_send()
    when_some(r, lambda: [users(k, lambda copy: copy.wait_send()) for k in range(homes)])

    def drain(i):
        h = target(i)

        def _():
            for w in range(2):
                for k in range(homes):
                    relay_copy(w, first(h) + k).wait_send()

        when_some(h, _)

    each(rows - 1, drain)
    for x in x_rows:
        x.wait()
    total = half_all[0]
    for o in range(1, rows):
        total = total + half_all[o]
    half_out[s] = total
    x_out = remote(half_out.at[s], half_out.at[s], sf_sem.at[0], sf_sem.at[1], g, r, c, other)
    x_out.start()
    x_out.wait()
    for o in range(subs):
        out[o * hq:(o + 1) * hq, :] = half_out[o]


def body(sizes, query_acts, query_grads, proj_in, proj_out, inverse_gram, store_slab):
    groups, rows, cols, subs = sizes
    queries, tokens, depth = query_acts.shape
    kin, kout = proj_in.shape[1], proj_out.shape[1]
    planes = cols * subs
    slices = groups * planes
    nq = planes * queries
    aw = kin // slices
    grows, gcols = inverse_gram.shape
    kw = gcols // groups
    mb = min(512, grows // subs)
    blocks = grows // mb
    per = blocks // subs
    spread = groups * cols
    examples = store_slab.shape[0]
    hq = nq // subs
    homes = -(-queries // rows)
    assert rows % 2 == 0 and subs == 2 and (queries % rows == 0 or rows % queries == 0)
    dma = pltpu.SemaphoreType.DMA
    lanes = -(-2 * groups * nq // 128) * 128
    scratch = [
        pltpu.VMEM(query_acts.shape, BF16), pltpu.VMEM(query_grads.shape, BF16),
        pltpu.VMEM(proj_in.shape, BF16), pltpu.VMEM(proj_out.shape, BF16),
        pltpu.VMEM((blocks, mb, kw), F32), pltpu.VMEM(store_slab.shape, BF16),
        pltpu.VMEM((2, queries, tokens, kin), F32), pltpu.VMEM((2, queries, tokens, kin), BF16),
        pltpu.VMEM((2, queries, tokens, kin), BF16), pltpu.VMEM((rows // 2, 2, homes, tokens, kin), BF16),
        pltpu.VMEM((homes, slices, aw, kout), BF16), pltpu.VMEM((queries, slices, aw, kout), BF16),
        pltpu.VMEM((slices, queries, aw, kout), F32), pltpu.VMEM((kw, lanes), BF16),
        pltpu.VMEM((per, groups * nq, mb), F32), pltpu.VMEM((per, groups * nq, mb), F32),
        pltpu.VMEM((per, groups, nq, mb), F32),
        pltpu.VMEM((per, groups, nq, mb), BF16), pltpu.VMEM((per, spread, nq, mb), BF16),
        pltpu.VMEM((subs, hq, examples), F32), pltpu.VMEM((hq, examples), F32), pltpu.VMEM((hq, examples), F32),
        pltpu.VMEM((rows, hq, examples), F32), pltpu.VMEM((subs, hq, examples), F32),
        dma((2,)), dma((rows, 2)), dma((blocks,)), dma((1,)), dma((2, queries)), dma((2, queries)),
        dma((rows // 2, 2, homes)), dma((homes, rows, slices)), dma((queries,)),
        dma((per,)), dma((per,)), dma((per, spread)), dma((per, spread)),
        dma((2,)), dma((rows,)), dma((rows,)), dma((2,)),
    ]
    return pl.pallas_call(
        functools.partial(kernel, groups, rows, cols, subs),
        out_shape=jax.ShapeDtypeStruct((nq, examples), F32),
        in_specs=[pl.BlockSpec(memory_space=pltpu.HBM)] * 6,
        out_specs=pl.BlockSpec(memory_space=pltpu.VMEM),
        scratch_shapes=scratch,
        compiler_params=pltpu.CompilerParams(
            collective_id=0, has_side_effects=True, vmem_limit_bytes=67043328),
        name="influence",
    )(query_acts, query_grads, proj_in, proj_out, inverse_gram, store_slab)


def solution(mesh):
    sizes = tuple(mesh.shape[n] for n in ("groups", "row", "col", "sub"))
    return jax.shard_map(
        functools.partial(body, sizes),
        mesh=mesh,
        in_specs=(
            P(("groups", "col", "sub"), None, "row"),
            P(("groups", "col", "sub"), None, "row"),
            P("row", None),
            P("row", None),
            P("row", ("col", "sub")),
            P(("groups", "col"), ("row", "sub")),
        ),
        out_specs=P("groups", "col"),
        check_vma=False,
    )
```

time: 58.4 us -> 51.1 us (0.88)
  Pallas kernels: 56.8 us -> 49.4 us
    pallas_call x1, Pallas kernels: 56.8 us -> 49.4 us  [body(): pl.pallas_call(functools.partial(kernel, groups, rows, cols, subs), out_s...]
where the time goes in v2:
time: 51.1 us; the launch traced here: 50.9 us
  Pallas kernels  49.4 us (97%)
  local copies, waits for them, and re-layouts  1.47 us (3%)
    pallas_call x1, Pallas kernels, body(): pl.pallas_call(functools.partial(kernel, groups, rows, cols, subs), out_s...  49.4 us
    unnamed x1, local copies, waits for them, and re-layouts  1.47 us

profile of v2, /device:TPU:0, one launch (start us, length us, event | category | flops | bytes accessed | tf_op | source)
XLA Modules:
  0.0 50.9 jit_solution(11712979802886602883)
XLA Ops:
  0.0 49.4 %influence.1 = f32[32,512]{1,0:T(8,128)} custom-call(bf16[8,128,1024]{2,1,0:T(8,128)(2,1)} %acts_h.1, bf16[8,128,1024]{2,1,0:T(8,128)(2,1)} %grads_h.1, bf16[1024,128]{1,0:T(8,128)(2,1)} %pin_h.1, bf16[1024,128]{1,0:T(8,128)(2,1)} %pout_h.1, f32[4096,4096]{1,0:T(8,128)} %gram_h.1, bf16[512,2048]{1,0:T(8,128)(2,1)} %store_h.1), custom_call_target="tpu_custom_call" | custom-call | tf_op jit(solution)/shard_map/influence/pallas_call | solution.py:393
  49.4 1.5 %copy.8 = f32[32,512]{1,0:T(8,128)} copy(f32[32,512]{1,0:T(8,128)} %influence.1) | data formatting | bytes 131072

commit v3 on v2

--- a/solution.py
+++ b/solution.py
@@ -9,7 +9,7 @@
 from jax.sharding import PartitionSpec as P
 
 F32, BF16 = jnp.float32, jnp.bfloat16
-ACT_MAX, GRAD_MAX, PROJ_MAX, GRAM_MAX = 6.0, 0.5390625, 0.09375, 2.01
+ACT_MAX, GRAD_MAX, PROJ_MAX, GRAM_MAX, STORE_MAX = 6.0, 0.5390625, 0.09375, 2.01, 0.046875
 
 
 def split(x):
@@ -79,7 +79,9 @@
     feat_bound = tokens * act_bound * grad_bound
     ps = scale_of(4, max(act_bound, grad_bound))
     fs = scale_of(3, feat_bound)
-    gs = scale_of(2, feat_bound * GRAM_MAX * gram_h.shape[1] * planes)
+    pre_bound = feat_bound * GRAM_MAX * gram_h.shape[1] * planes
+    gs = scale_of(2, pre_bound)
+    zs = scale_of(2, pre_bound * STORE_MAX * gram_h.shape[1] * planes)
 
     def dev(group, row, col, sub):
         return {"groups": group, "row": row, "col": col, "sub": sub}
@@ -126,6 +128,17 @@
     for w in range(2):
         loads[w].start()
         when_some(target(0), lambda: load(target(0), w).start())
+
+    barrier = pltpu.get_barrier_semaphore()
+
+    def greet(*place):
+        pl.semaphore_signal(barrier, inc=1, device_id=dev(*place), device_id_type=pl.DeviceIdType.MESH)
+
+    for d in range(1, slices):
+        greet(*at_spot(lax.rem(spot + d, slices), r))
+    for d in range(1, rows):
+        greet(g, lax.rem(r + d, rows), c, s)
+    guests = slices - 1 + rows - 1
 
     def more(i):
         h = target(i + 1)
@@ -140,16 +153,6 @@
             gram.at[n], gram_sem.at[n])
 
     store_copy = pltpu.make_async_copy(store_h, store, store_sem.at[0])
-
-    barrier = pltpu.get_barrier_semaphore()
-    everyone = rows * slices
-
-    def greet(d):
-        o = lax.rem(r * slices + spot + d + 1, everyone)
-        group, row, col, sub = at_spot(lax.rem(o, slices), o // slices)
-        pl.semaphore_signal(barrier, inc=1, device_id=dev(group, row, col, sub), device_id_type=pl.DeviceIdType.MESH)
-
-    lax.fori_loop(0, everyone - 1, lambda d, z: (greet(d), z)[1], 0)
 
     def relay_copy(w, q):
         return remote(send.at[w, q], relay.at[w, q], rs_send.at[w, q], rl_recv.at[w, q], g, partner, c, s)
@@ -171,7 +174,7 @@
                                 preferred_element_type=F32).reshape(homes, tokens, kin)
                 part[w, q] = value
                 if isinstance(i, int) and i == 0 and w == 0:
-                    pl.semaphore_wait(barrier, everyone - 1)
+                    pl.semaphore_wait(barrier, guests)
 
                 @pl.when(jnp.logical_not(jnp.logical_or(h == r, relays(h))))
                 def _():
@@ -190,7 +193,7 @@
     if rows > 8:
         for l in loads:
             l.wait()
-        pl.semaphore_wait(barrier, everyone - 1)
+        pl.semaphore_wait(barrier, guests)
     each(rows, project)
     for n in range(blocks):
         gram_copy(n).start()
@@ -223,19 +226,21 @@
         return pltpu.make_async_copy(fsend.at[k, spot], fbuf.at[first(r) + k, source], fx_recv.at[first(r) + k])
 
     def users(k, use):
-        def row_of(j):
-            row = jnp.where(2 * r < rows, rows - 1 - j, j)
-
-            def slice_of(d):
-                o = lax.rem(spot + d, slices)
-
-                @pl.when(jnp.logical_or(row != r, o != spot))
-                def _():
+        def slice_of(d):
+            o = lax.rem(spot + d + 1, slices)
+
+            def row_of(j):
+                row = jnp.where(2 * r < rows, rows - 1 - j, j)
+                if isinstance(d, int) and d < slices - 1:
                     use(fx_copy(k, row, o))
-
-            each(slices, slice_of)
-
-        each(rows, row_of)
+                else:
+                    @pl.when(jnp.logical_or(row != r, o != spot))
+                    def _():
+                        use(fx_copy(k, row, o))
+
+            each(rows, row_of)
+
+        each(slices, slice_of)
 
     def final():
         for k in range(homes):
@@ -288,16 +293,24 @@
         t = acc.T
         return t[:allq] + t[allq:2 * allq]
 
-    for p in range(per):
+    def theirs(p):
         pre[p] = product(subs * p)
         sub_copy(p).start()
-        value = product(subs * p + 1)
+
+    def combine(p):
         sub_copy(p).wait_recv()
-        value = (value + sub_in[p]).reshape(groups, nq, mb)
+        value = (tot[p] + sub_in[p].reshape(groups, nq, mb))
         tot[p] = value
         vsend[p] = encode(value, 2, gs)
         for d in range(1, spread):
             v_copy(p, d).start()
+
+    theirs(0)
+    for p in range(per):
+        if p + 1 < per:
+            theirs(p + 1)
+        tot[p] = product(subs * p + 1).reshape(groups, nq, mb)
+        combine(p)
     store_copy.wait()
     score = None
     for p in range(per):
@@ -316,12 +329,13 @@
     x_half = remote(own.at[other], half_in, ss_sem.at[0], ss_sem.at[1], g, r, c, other)
     x_half.start()
     x_half.wait()
-    own_s[...] = own[s] + half_in[...]
-    x_rows = [remote(own_s, half_all.at[r], sz_send.at[d], sz_recv.at[d], g, lax.rem(r + d, rows), c, s)
+    half = own[s] + half_in[...]
+    own_s[...] = encode(half, 2, zs)
+    x_rows = [remote(own_s, half_all.at[d], sz_send.at[d], sz_recv.at[d], g, lax.rem(r + d, rows), c, s)
               for d in range(1, rows)]
     for x in x_rows:
         x.start()
-    half_all[r] = own_s[...]
+    half_in[...] = half
     for p in range(per):
         sub_copy(p).wait_send()
         for d in range(1, spread):
@@ -339,11 +353,10 @@
         when_some(h, _)
 
     each(rows - 1, drain)
-    for x in x_rows:
-        x.wait()
-    total = half_all[0]
-    for o in range(1, rows):
-        total = total + half_all[o]
+    total = half_in[...]
+    for d in range(1, rows):
+        x_rows[d - 1].wait()
+        total = total + decode(half_all[d], 2, zs)
     half_out[s] = total
     x_out = remote(half_out.at[s], half_out.at[s], sf_sem.at[0], sf_sem.at[1], g, r, c, other)
     x_out.start()
@@ -383,8 +396,8 @@
         pltpu.VMEM((per, groups * nq, mb), F32), pltpu.VMEM((per, groups * nq, mb), F32),
         pltpu.VMEM((per, groups, nq, mb), F32),
         pltpu.VMEM((per, groups, nq, mb), BF16), pltpu.VMEM((per, spread, nq, mb), BF16),
-        pltpu.VMEM((subs, hq, examples), F32), pltpu.VMEM((hq, examples), F32), pltpu.VMEM((hq, examples), F32),
-        pltpu.VMEM((rows, hq, examples), F32), pltpu.VMEM((subs, hq, examples), F32),
+        pltpu.VMEM((subs, hq, examples), F32), pltpu.VMEM((hq, examples), BF16), pltpu.VMEM((hq, examples), F32),
+        pltpu.VMEM((rows, hq, examples), BF16), pltpu.VMEM((subs, hq, examples), F32),
         dma((2,)), dma((rows, 2)), dma((blocks,)), dma((1,)), dma((2, queries)), dma((2, queries)),
         dma((rows // 2, 2, homes)), dma((homes, rows, slices)), dma((queries,)),
         dma((per,)), dma((per,)), dma((per, spread)), dma((per, spread)),

time: 51.1 us -> 48.1 us (0.941)
  Pallas kernels: 49.4 us -> 46.5 us
    pallas_call x1, Pallas kernels: 49.4 us -> 46.5 us  [body(): pl.pallas_call(functools.partial(kernel, groups, rows, cols, subs), out_s...]
where the time goes in v3:
time: 48.1 us; the launch traced here: 48 us
  Pallas kernels  46.5 us (97%)
  local copies, waits for them, and re-layouts  1.47 us (3%)
    pallas_call x1, Pallas kernels, body(): pl.pallas_call(functools.partial(kernel, groups, rows, cols, subs), out_s...  46.5 us
    unnamed x1, local copies, waits for them, and re-layouts  1.47 us

profile of v3, /device:TPU:0, one launch (start us, length us, event | category | flops | bytes accessed | tf_op | source)
XLA Modules:
  0.0 48.0 jit_solution(13536340070935589282)
XLA Ops:
  0.0 46.5 %influence.1 = f32[32,512]{1,0:T(8,128)} custom-call(bf16[8,128,1024]{2,1,0:T(8,128)(2,1)} %acts_h.1, bf16[8,128,1024]{2,1,0:T(8,128)(2,1)} %grads_h.1, bf16[1024,128]{1,0:T(8,128)(2,1)} %pin_h.1, bf16[1024,128]{1,0:T(8,128)(2,1)} %pout_h.1, f32[4096,4096]{1,0:T(8,128)} %gram_h.1, bf16[512,2048]{1,0:T(8,128)(2,1)} %store_h.1), custom_call_target="tpu_custom_call" | custom-call | tf_op jit(solution)/shard_map/influence/pallas_call | solution.py:406
  46.5 1.5 %copy.8 = f32[32,512]{1,0:T(8,128)} copy(f32[32,512]{1,0:T(8,128)} %influence.1) | data formatting | bytes 131072

commit v4 on v3

--- a/solution.py
+++ b/solution.py
@@ -56,7 +56,7 @@
 
 
 def kernel(groups, rows, cols, subs, acts_h, grads_h, pin_h, pout_h, gram_h, store_h, out,
-           acts, grads, pin, pout, gram, store, part, send, relay, recv, fsend, fbuf, feats, ft,
+           acts, grads, pin, pout, gram, store, part, send, relay, recv, fsend, fbuf, feats, ft, early,
            pre, sub_in, tot, vsend, vin, own, own_s, half_in, half_all, half_out,
            p_sem, in_sem, gram_sem, store_sem, rs_send, rl_recv, rh_recv, fx_send, fx_recv,
            ps_send, ps_recv, pv_send, pv_recv, ss_sem, sz_send, sz_recv, sf_sem):
@@ -73,7 +73,8 @@
     per = blocks // subs
     other = lax.rem(s + 1, subs)
     nq = planes * queries
-    homes = fsend.shape[0]
+    parts, _, homes, az, _ = fsend.shape
+    kz = kw // parts
     act_bound = rows * depth * ACT_MAX * PROJ_MAX
     grad_bound = rows * depth * GRAD_MAX * PROJ_MAX
     feat_bound = tokens * act_bound * grad_bound
@@ -218,25 +219,27 @@
 
     each(rows - 1, forward)
 
-    def fx_copy(k, row, o):
-        return remote(fsend.at[k, o], fbuf.at[first(r) + k, source], fx_send.at[k, row, o],
-                      fx_recv.at[first(r) + k], *at_spot(o, row))
-
-    def fx_own(k):
-        return pltpu.make_async_copy(fsend.at[k, spot], fbuf.at[first(r) + k, source], fx_recv.at[first(r) + k])
-
-    def users(k, use):
+    unit = first(r) // homes
+
+    def fx_copy(z, row, o):
+        return remote(fsend.at[z, o], fbuf.at[z, unit, source], fx_send.at[z, row, o], fx_recv.at[z, unit],
+                      *at_spot(o, row))
+
+    def fx_own(z):
+        return pltpu.make_async_copy(fsend.at[z, spot], fbuf.at[z, unit, source], fx_recv.at[z, unit])
+
+    def users(z, use):
         def slice_of(d):
             o = lax.rem(spot + d + 1, slices)
 
             def row_of(j):
                 row = jnp.where(2 * r < rows, rows - 1 - j, j)
                 if isinstance(d, int) and d < slices - 1:
-                    use(fx_copy(k, row, o))
+                    use(fx_copy(z, row, o))
                 else:
                     @pl.when(jnp.logical_or(row != r, o != spot))
                     def _():
-                        use(fx_copy(k, row, o))
+                        use(fx_copy(z, row, o))
 
             each(rows, row_of)
 
@@ -257,24 +260,29 @@
             gh, gl = split(sides[1])
             f = jnp.dot(jnp.concatenate([ah, al, ah], axis=1), jnp.concatenate([gh, gh, gl], axis=0),
                         preferred_element_type=F32)
-            fsend[k] = encode(f.reshape(slices, aw, kout), 3, fs)
-            users(k, lambda copy: copy.start())
-            fx_own(k).start()
+            f = f.reshape(slices, aw, kout)
+            for z in range(parts):
+                fsend[z, :, k] = encode(f[:, z * az:(z + 1) * az], 3, fs)
+        for z in range(parts):
+            users(z, lambda copy: copy.start())
+            fx_own(z).start()
 
     when_some(r, final)
-
-    for q in range(queries):
-        remote(fbuf.at[q], fbuf.at[q], fx_send.at[0, 0, 0], fx_recv.at[q], g, partner, c, s).wait_recv()
-        feats[:, q] = decode(fbuf[q], 3, fs)
 
     width = ft.shape[1]
     allq = groups * nq
-    for a in range(aw):
-        x = feats[:, :, a, :].reshape(allq, kout)
-        xh, xl = split(x)
-        rest = [jnp.zeros((width - 2 * allq, kout), F32)] if width > 2 * allq else []
-        y = jnp.concatenate([xh.astype(F32), xl.astype(F32)] + rest, axis=0)
-        ft[a * kout:(a + 1) * kout, :] = y.T.astype(BF16)
+
+    def take(z):
+        for u in range(queries // homes):
+            remote(fbuf.at[z, u], fbuf.at[z, u], fx_send.at[0, 0, 0], fx_recv.at[z, u], g, partner, c, s).wait_recv()
+            for k in range(homes):
+                feats[:, u * homes + k, z * az:(z + 1) * az] = decode(fbuf[z, u, :, k], 3, fs)
+        for a in range(z * az, (z + 1) * az):
+            x = feats[:, :, a, :].reshape(allq, kout)
+            xh, xl = split(x)
+            rest = [jnp.zeros((width - 2 * allq, kout), F32)] if width > 2 * allq else []
+            y = jnp.concatenate([xh.astype(F32), xl.astype(F32)] + rest, axis=0)
+            ft[a * kout:(a + 1) * kout, :] = y.T.astype(BF16)
 
     def sub_copy(p):
         return remote(pre.at[p], sub_in.at[p], ps_send.at[p], ps_recv.at[p], g, r, c, other)
@@ -288,8 +296,9 @@
                       o // cols, r, lax.rem(o, cols), s)
 
     def product(n):
-        gram_copy(n).wait()
-        acc = jnp.dot(gram[n].astype(BF16), ft[...], preferred_element_type=F32)
+        acc = jnp.dot(gram[n, :, kw - kz:].astype(BF16), ft[kw - kz:], preferred_element_type=F32)
+        if parts > 1:
+            acc = acc + early[n]
         t = acc.T
         return t[:allq] + t[allq:2 * allq]
 
@@ -305,6 +314,15 @@
         for d in range(1, spread):
             v_copy(p, d).start()
 
+    for n in range(blocks):
+        gram_copy(n).wait()
+    for z in range(parts):
+        take(z)
+        if z < parts - 1:
+            for n in range(0, blocks, 2):
+                acc = jnp.dot(gram[n:n + 2, :, z * kz:(z + 1) * kz].reshape(2 * mb, kz).astype(BF16),
+                              ft[z * kz:(z + 1) * kz], preferred_element_type=F32).reshape(2, mb, width)
+                early[n:n + 2] = acc + early[n:n + 2] if z else acc
     theirs(0)
     for p in range(per):
         if p + 1 < per:
@@ -340,7 +358,8 @@
         sub_copy(p).wait_send()
         for d in range(1, spread):
             v_copy(p, d).wait_send()
-    when_some(r, lambda: [users(k, lambda copy: copy.wait_send()) for k in range(homes)])
+    for z in range(parts):
+        when_some(r, lambda: users(z, lambda copy: copy.wait_send()))
 
     def drain(i):
         h = target(i)
@@ -385,21 +404,24 @@
     assert rows % 2 == 0 and subs == 2 and (queries % rows == 0 or rows % queries == 0)
     dma = pltpu.SemaphoreType.DMA
     lanes = -(-2 * groups * nq // 128) * 128
+    parts = 2 if aw % 16 == 0 else 1
     scratch = [
         pltpu.VMEM(query_acts.shape, BF16), pltpu.VMEM(query_grads.shape, BF16),
         pltpu.VMEM(proj_in.shape, BF16), pltpu.VMEM(proj_out.shape, BF16),
         pltpu.VMEM((blocks, mb, kw), F32), pltpu.VMEM(store_slab.shape, BF16),
         pltpu.VMEM((2, queries, tokens, kin), F32), pltpu.VMEM((2, queries, tokens, kin), BF16),
         pltpu.VMEM((2, queries, tokens, kin), BF16), pltpu.VMEM((rows // 2, 2, homes, tokens, kin), BF16),
-        pltpu.VMEM((homes, slices, aw, kout), BF16), pltpu.VMEM((queries, slices, aw, kout), BF16),
+        pltpu.VMEM((parts, slices, homes, aw // parts, kout), BF16),
+        pltpu.VMEM((parts, queries // homes, slices, homes, aw // parts, kout), BF16),
         pltpu.VMEM((slices, queries, aw, kout), F32), pltpu.VMEM((kw, lanes), BF16),
+        pltpu.VMEM((blocks, mb, lanes) if parts > 1 else (1, 8, 128), F32),
         pltpu.VMEM((per, groups * nq, mb), F32), pltpu.VMEM((per, groups * nq, mb), F32),
         pltpu.VMEM((per, groups, nq, mb), F32),
         pltpu.VMEM((per, groups, nq, mb), BF16), pltpu.VMEM((per, spread, nq, mb), BF16),
         pltpu.VMEM((subs, hq, examples), F32), pltpu.VMEM((hq, examples), BF16), pltpu.VMEM((hq, examples), F32),
         pltpu.VMEM((rows, hq, examples), BF16), pltpu.VMEM((subs, hq, examples), F32),
         dma((2,)), dma((rows, 2)), dma((blocks,)), dma((1,)), dma((2, queries)), dma((2, queries)),
-        dma((rows // 2, 2, homes)), dma((homes, rows, slices)), dma((queries,)),
+        dma((rows // 2, 2, homes)), dma((parts, rows, slices)), dma((parts, queries // homes)),
         dma((per,)), dma((per,)), dma((per, spread)), dma((per, spread)),
         dma((2,)), dma((rows,)), dma((rows,)), dma((2,)),
     ]
@@ -410,9 +432,9 @@
         out_specs=pl.BlockSpec(memory_space=pltpu.VMEM),
         scratch_shapes=scratch,
         compiler_params=pltpu.CompilerParams(
-            collective_id=0, has_side_effects=True, vmem_limit_bytes=67043328),
+            collective_id=0, has_side_effects=True, vmem_limit_bytes=50 << 20),
         name="influence",
-    )(query_acts, query_grads, proj_in, proj_out, inverse_gram, store_slab)
+    )(*(pltpu.with_memory_space_constraint(a, pltpu.HBM) for a in (query_acts, query_grads, proj_in, proj_out, inverse_gram, store_slab)))
 
 
 def solution(mesh):

time: 48.1 us -> 44 us (0.915)
  Pallas kernels: 46.5 us -> 43.2 us
  local copies, waits for them, and re-layouts: 1.47 us -> 0.63 us
    pallas_call x1, Pallas kernels: 46.5 us -> 43.2 us  [body(): pl.pallas_call(functools.partial(kernel, groups, rows, cols, subs), out_s...]
    unnamed x1, local copies, waits for them, and re-layouts: 1.47 us -> 0.63 us
where the time goes in v4:
time: 44 us; the launch traced here: 43.9 us
  Pallas kernels  43.2 us (98%)
  local copies, waits for them, and re-layouts  0.63 us (1%)
    pallas_call x1, Pallas kernels, body(): pl.pallas_call(functools.partial(kernel, groups, rows, cols, subs), out_s...  43.2 us

profile of v4, /device:TPU:0, one launch (start us, length us, event | category | flops | bytes accessed | tf_op | source)
XLA Modules:
  0.0 43.9 jit_solution(6703779351203763004)
XLA Ops:
  0.0 43.2 %influence.1 = f32[32,512]{1,0:T(8,128)S(1)} custom-call(bf16[8,128,1024]{2,1,0:T(8,128)(2,1)} %acts_h.1, bf16[8,128,1024]{2,1,0:T(8,128)(2,1)} %grads_h.1, bf16[1024,128]{1,0:T(8,128)(2,1)} %pin_h.1, bf16[1024,128]{1,0:T(8,128)(2,1)} %pout_h.1, f32[4096,4096]{1,0:T(8,128)} %gram_h.1, bf16[512,2048]{1,0:T(8,128)(2,1)} %store_h.1), custom_call_target="tpu_custom_call" | custom-call | tf_op jit(solution)/shard_map/influence/pallas_call | solution.py:428
  43.2 0.6 %copy.8 = f32[32,512]{1,0:T(8,128)} copy(f32[32,512]{1,0:T(8,128)S(1)} %influence.1) | data formatting | bytes 131072

commit v5 on v4

--- a/solution.py
+++ b/solution.py
@@ -57,9 +57,9 @@
 
 def kernel(groups, rows, cols, subs, acts_h, grads_h, pin_h, pout_h, gram_h, store_h, out,
            acts, grads, pin, pout, gram, store, part, send, relay, recv, fsend, fbuf, feats, ft, early,
-           pre, sub_in, tot, vsend, vin, own, own_s, half_in, half_all, half_out,
+           pre, sub_in, tot, vsend, vin, own, own_s, half_in, half_all,
            p_sem, in_sem, gram_sem, store_sem, rs_send, rl_recv, rh_recv, fx_send, fx_recv,
-           ps_send, ps_recv, pv_send, pv_recv, ss_sem, sz_send, sz_recv, sf_sem):
+           ps_send, ps_recv, pv_send, pv_recv, ss_sem, sz_send, sz_recv):
     g, r, c, s = (lax.axis_index(n) for n in ("groups", "row", "col", "sub"))
     queries, tokens, depth = acts.shape
     planes = cols * subs
@@ -349,8 +349,11 @@
     x_half.wait()
     half = own[s] + half_in[...]
     own_s[...] = encode(half, 2, zs)
-    x_rows = [remote(own_s, half_all.at[d], sz_send.at[d], sz_recv.at[d], g, lax.rem(r + d, rows), c, s)
-              for d in range(1, rows)]
+    ring = rows * subs
+    x_rows = []
+    for d in range(1, ring):
+        o = lax.rem(r * subs + s + d, ring)
+        x_rows.append(remote(own_s, half_all.at[d], sz_send.at[d], sz_recv.at[d], g, o // subs, c, lax.rem(o, subs)))
     for x in x_rows:
         x.start()
     half_in[...] = half
@@ -372,16 +375,13 @@
         when_some(h, _)
 
     each(rows - 1, drain)
-    total = half_in[...]
-    for d in range(1, rows):
+    totals = [half_in[...], None]
+    for d in range(1, ring):
         x_rows[d - 1].wait()
-        total = total + decode(half_all[d], 2, zs)
-    half_out[s] = total
-    x_out = remote(half_out.at[s], half_out.at[s], sf_sem.at[0], sf_sem.at[1], g, r, c, other)
-    x_out.start()
-    x_out.wait()
-    for o in range(subs):
-        out[o * hq:(o + 1) * hq, :] = half_out[o]
+        part_d = decode(half_all[d], 2, zs)
+        totals[d % subs] = part_d if totals[d % subs] is None else totals[d % subs] + part_d
+    for o, total in zip((s, other), totals):
+        out[pl.ds(pl.multiple_of(o * hq, hq), hq), :] = total
 
 
 def body(sizes, query_acts, query_grads, proj_in, proj_out, inverse_gram, store_slab):
@@ -419,11 +419,11 @@
         pltpu.VMEM((per, groups, nq, mb), F32),
         pltpu.VMEM((per, groups, nq, mb), BF16), pltpu.VMEM((per, spread, nq, mb), BF16),
         pltpu.VMEM((subs, hq, examples), F32), pltpu.VMEM((hq, examples), BF16), pltpu.VMEM((hq, examples), F32),
-        pltpu.VMEM((rows, hq, examples), BF16), pltpu.VMEM((subs, hq, examples), F32),
+        pltpu.VMEM((rows * subs, hq, examples), BF16),
         dma((2,)), dma((rows, 2)), dma((blocks,)), dma((1,)), dma((2, queries)), dma((2, queries)),
         dma((rows // 2, 2, homes)), dma((parts, rows, slices)), dma((parts, queries // homes)),
         dma((per,)), dma((per,)), dma((per, spread)), dma((per, spread)),
-        dma((2,)), dma((rows,)), dma((rows,)), dma((2,)),
+        dma((2,)), dma((rows * subs,)), dma((rows * subs,)),
     ]
     return pl.pallas_call(
         functools.partial(kernel, groups, rows, cols, subs),

time: 44 us -> 43.4 us (0.986)
  Pallas kernels: 43.2 us -> 42.6 us
    pallas_call x1, Pallas kernels: 43.2 us -> 42.6 us  [body(): pl.pallas_call(functools.partial(kernel, groups, rows, cols, subs), out_s...]
where the time goes in v5:
time: 43.4 us; the launch traced here: 43.2 us
  Pallas kernels  42.6 us (98%)
  local copies, waits for them, and re-layouts  0.63 us (1%)
    pallas_call x1, Pallas kernels, body(): pl.pallas_call(functools.partial(kernel, groups, rows, cols, subs), out_s...  42.6 us

profile of v5, /device:TPU:0, one launch (start us, length us, event | category | flops | bytes accessed | tf_op | source)
XLA Modules:
  0.0 43.2 jit_solution(13478945038167901951)
XLA Ops:
  0.0 42.6 %influence.1 = f32[32,512]{1,0:T(8,128)S(1)} custom-call(bf16[8,128,1024]{2,1,0:T(8,128)(2,1)} %acts_h.1, bf16[8,128,1024]{2,1,0:T(8,128)(2,1)} %grads_h.1, bf16[1024,128]{1,0:T(8,128)(2,1)} %pin_h.1, bf16[1024,128]{1,0:T(8,128)(2,1)} %pout_h.1, f32[4096,4096]{1,0:T(8,128)} %gram_h.1, bf16[512,2048]{1,0:T(8,128)(2,1)} %store_h.1), custom_call_target="tpu_custom_call" | custom-call | tf_op jit(solution)/shard_map/influence/pallas_call | solution.py:428
  42.6 0.6 %copy.8 = f32[32,512]{1,0:T(8,128)} copy(f32[32,512]{1,0:T(8,128)S(1)} %influence.1) | data formatting | bytes 131072
